TPU v7x, 32 devices: a whole 2x2x4 slice. The times are simulated.
32 devices in a mesh: wide: 8 (over z, x), narrow: 4 (over y, core).
Axes of the slice: x: 2, y: 2, z: 4, core: 2. Of those that a mesh axis runs over, the one named last changes fastest.
Arguments:
- embeddings: bfloat16 [16384, 1024], P(('wide', 'narrow')), may hold values from -32 to 32
- valid: int32 [16384], P(('wide', 'narrow')), may hold values from 0 to 1, as said below
Outputs:
- whitened: bfloat16 [16384, 1024], P(('wide', 'narrow'))
Inputs may be any that keep to these rules, and one draw needn't show every extreme that they name: The first row of every aligned block of 16 rows has valid = 1.
All inputs are finite; a program needn't handle non-finite values.
Results may differ from a plain program's by a relative error of at most 0.001.
Values sent between devices are 32-bit elements; how exact they have to be, the bound alone decides.
No kernel may reach another device: no remote copies, remote signals or barrier semaphores. Data moves between devices by JAX's collectives and lax.ppermute only.
A program may use at most 64 MiB of HBM per device.

v0:
```python
import jax
import jax.numpy as jnp
from jax import lax
from jax.sharding import PartitionSpec as P


def shifted_scatter(gram, count_local, sums_local, center):
    return (
        gram
        - sums_local[:, None] * center[None, :]
        - center[:, None] * sums_local[None, :]
        + count_local * center[:, None] * center[None, :]
    )


def narrow_rows(term):
    return lax.psum_scatter(term, "narrow", scatter_dimension=0, tiled=True)


def on_device(embeddings, valid):
    width = embeddings.shape[1]
    narrow_count = lax.axis_size("narrow")
    row_span = width // narrow_count
    offset = lax.axis_index("narrow") * row_span
    mask_half = valid.astype(jnp.bfloat16)
    count_local = jnp.sum(valid.astype(jnp.float32))
    masked = embeddings * mask_half[:, None]
    gram = lax.dot_general(
        masked, embeddings, (((0,), (0,)), ((), ())), preferred_element_type=jnp.float32
    )
    sums_local = jnp.dot(mask_half[None, :], embeddings, preferred_element_type=jnp.float32)[0]
    count, sums = lax.psum((count_local, sums_local), ("wide", "narrow"))
    term = shifted_scatter(gram, count_local, sums_local, sums / count)
    level_rows = narrow_rows(term)
    own_rows = lax.psum(level_rows, "wide")
    center = sums / count
    cov_rows = own_rows / count
    ident_rows = (
        lax.broadcasted_iota(jnp.int32, (row_span, width), 0) + offset
        == lax.broadcasted_iota(jnp.int32, (row_span, width), 1)
    ).astype(jnp.float32)
    diag_block = lax.dynamic_slice_in_dim(cov_rows, offset, row_span, 1)
    trace_part = jnp.sum(jnp.diagonal(diag_block))
    square_part = jnp.sum(cov_rows * cov_rows)
    trace_cov, square_sum = lax.psum((trace_part, square_part), "narrow")
    ridge_add = 0.05 * trace_cov / width + 1e-06
    norm_frob = jnp.sqrt(square_sum + 2.0 * ridge_add * trace_cov + width * ridge_add * ridge_add)
    base_rows = (cov_rows + ridge_add * ident_rows) / norm_frob
    root_rows = (3.0 * ident_rows - base_rows) / 2.0
    root_full = lax.all_gather(root_rows, "narrow", axis=0, tiled=True)
    first = jnp.dot(
        base_rows, root_full, precision=lax.Precision.HIGHEST, preferred_element_type=jnp.float32
    )
    second = jnp.dot(
        first, root_full, precision=lax.Precision.HIGHEST, preferred_element_type=jnp.float32
    )
    factor = (3.0 * ident_rows - second) / 2.0
    root_rows = jnp.dot(
        factor, root_full, precision=lax.Precision.HIGHEST, preferred_element_type=jnp.float32
    )
    centered_x = embeddings.astype(jnp.float32) - center
    product = jnp.dot(
        centered_x,
        lax.all_gather(root_rows, "narrow", axis=0, tiled=True),
        precision=lax.Precision.HIGHEST,
        preferred_element_type=jnp.float32,
    )
    return (product / jnp.sqrt(norm_frob)).astype(jnp.bfloat16)


def solution(mesh):
    in_specs = (P(("wide", "narrow"), None), P(("wide", "narrow")))
    out_specs = P(("wide", "narrow"), None)
    return jax.shard_map(
        on_device, mesh=mesh, in_specs=in_specs, out_specs=out_specs, check_vma=False
    )
```

profile of v0, /device:TPU:0, one launch (start us, length us, event | category | flops | bytes accessed | tf_op | source)
XLA Modules:
  0.0 300.6 jit_solution(4755402428084836865)
XLA Ops:
  6.5 0.7 convert_element_type.14
  7.2 1.3 convert_reduce_fusion
  8.5 1.5 fusion.11
  10.0 42.1 %all-reduce = (f32[1024]{0:T(1024)S(1)}, f32[]{:T(128)}) all-reduce(f32[1024]{0:T(1024)S(1)} %bitcast.12, f32[]{:T(128)} %convert_reduce_fusion), channel_id=1, replica_groups=mesh['wide'=8,'narrow'=4] {'wide','narrow'}, use_global_device_ids=true, to_apply=%region_0.0 | all-reduce | flops 1025 | bytes 8200 | tf_op jit(solution)/shard_map/psum | solution.py:32
  52.1 1.3 broadcast_multiply_fusion
  53.4 5.3 %multiply_add_fusion = f32[1024,1024]{1,0:T(8,128)} fusion(bf16[512,1024]{1,0:T(8,128)(2,1)} %param.2, f32[1024]{0:T(1024)S(1)} %get-tuple-element.11, f32[1024]{0:T(1024)S(1)} %bitcast.13, f32[1024]{0:T(1024)S(1)} %get-tuple-element.12, bf16[512]{0:T(512)(128)(2,1)S(1)} %convert_element_type.14), kind=kOutput, calls=%fused_computation.1 | convolution fusion | flops 1080557568 | bytes 5256192 | tf_op jit(solution)/shard_map/dot_general | solution.py:28
  58.7 0.0 all-reduce.4.cloned.1.call-start
  58.8 44.7 %reduce-scatter.2.cloned.1.call-done = f32[256,1024]{1,0:T(8,128)} async-done(((f32[1024,1024]{1,0:T(8,128)}), f32[256,1024]{1,0:T(8,128)}) %reduce-scatter.2.cloned.1.call-update) | async-done | bytes 1048592 | tf_op jit(solution)/shard_map/reduce_scatter | solution.py:17
  103.5 0.0 all-reduce.4.cloned.1.call-update
  103.5 0.0 all-gather.3.cloned.1.call-start
  103.6 81.6 %all-reduce.4.cloned.1.call-done = f32[256,1024]{1,0:T(8,128)} async-done(((f32[256,1024]{1,0:T(8,128)}), f32[256,1024]{1,0:T(8,128)}) %all-reduce.4.cloned.1.call-update) | async-done | bytes 1048592 | tf_op jit(solution)/shard_map/psum | solution.py:35
  185.2 2.7 multiply_reduce_fusion
  188.0 2.3 gather_fusion
  190.4 0.7 reduce_sum.28
  191.0 7.2 %all-reduce.1 = (f32[]{:T(128)}, f32[]{:T(128)}) all-reduce(f32[]{:T(128)} %get-tuple-element.9, f32[]{:T(128)} %reduce_sum.28), channel_id=1, replica_groups=mesh['wide'=8,'narrow'=4] {'narrow'}, use_global_device_ids=true, to_apply=%region_8.9 | all-reduce | flops 2 | bytes 16 | tf_op jit(solution)/shard_map/psum | solution.py:45
  200.3 1.3 fusion.7
  201.6 0.0 all-gather.3.cloned.1.call-update
  201.6 0.2 all-gather.5.cloned.1.call-start
  201.8 33.4 %all-gather.3.cloned.1.call-done = f32[1024,1024]{1,0:T(8,128)} async-done(((f32[256,1024]{1,0:T(8,128)}), f32[1024,1024]{1,0:T(8,128)}) %all-gather.3.cloned.1.call-update) | async-done | bytes 4194320 | tf_op jit(solution)/shard_map/all_gather | solution.py:50
  235.2 6.1 %fusion.10 = f32[256,1024]{1,0:T(8,128)S(1)} fusion(f32[1024,1024]{1,0:T(8,128)} %all-gather.3.cloned.1.call-done, f32[256,1024]{1,0:T(8,128)S(1)} %get-tuple-element.10, f32[]{:T(128)S(6)} %sqrt.6, f32[]{:T(128)S(6)} %add.45, s32[256]{0:T(256)S(1)} %iota_add_fusion), kind=kOutput, calls=%fused_computation.23 | convolution fusion | flops 3222274048 | bytes 6292488 | tf_op jit(solution)/shard_map/dot_general | solution.py:51
  241.4 3.7 %fusion.4 = f32[256,1024]{1,0:T(8,128)S(1)} fusion(f32[256,1024]{1,0:T(8,128)S(1)} %fusion.10, f32[1024,1024]{1,0:T(8,128)S(1)} %copy-done, s32[256]{0:T(256)S(1)} %iota_add_fusion), kind=kOutput, calls=%fused_computation.9 | convolution fusion | flops 3222274048 | bytes 6292480 | tf_op jit(solution)/shard_map/dot_general | solution.py:54
  245.2 4.7 %fusion.12 = f32[256,1024]{1,0:T(8,128)} fusion(f32[256,1024]{1,0:T(8,128)S(1)} %fusion.4, f32[1024,1024]{1,0:T(8,128)S(1)} %copy-done), kind=kOutput, calls=%fused_computation.25 | convolution fusion | flops 3221225472 | bytes 6291456 | tf_op jit(solution)/shard_map/dot_general | solution.py:58
  249.9 34.6 %all-gather.5.cloned.1.call-done = f32[1024,1024]{1,0:T(8,128)} async-done(((f32[256,1024]{1,0:T(8,128)}), f32[1024,1024]{1,0:T(8,128)}) %all-gather.5.cloned.1.call-update) | async-done | bytes 4194320 | tf_op jit(solution)/shard_map/all_gather | solution.py:64
  284.5 9.6 %divide_convert_fusion = bf16[512,1024]{1,0:T(8,128)(2,1)} fusion(f32[1024,1024]{1,0:T(8,128)} %all-gather.5.cloned.1.call-done, bf16[512,1024]{1,0:T(8,128)(2,1)S(1)} %copy-done.1, f32[]{:T(128)S(6)} %sqrt.7, f32[1024]{0:T(1024)S(1)} %get-tuple-element.12), kind=kOutput, calls=%fused_computation.2 | convolution fusion | flops 6444548096 | bytes 6295556 | tf_op jit(solution)/shard_map/dot_general | solution.py:62
  (11 shorter events, 0.1 us)
Async XLA Ops:
  6.5 97.0 %reduce-scatter.2.cloned.1.call-start = ((), (), s32[]{:S(2)}) async-start(), calls=%async_computation.1 | async-start | bytes 5242880 | tf_op jit(solution)/shard_map/reduce_scatter | solution.py:17
  58.7 126.5 %all-reduce.4.cloned.1.call-start = ((), (), s32[]{:S(2)}) async-start(), calls=%async_computation.2 | async-start | bytes 2097152 | tf_op jit(solution)/shard_map/psum | solution.py:35
  103.5 131.7 %all-gather.3.cloned.1.call-start = ((), (), s32[]{:S(2)}) async-start(), calls=%async_computation.3 | async-start | bytes 5242880 | tf_op jit(solution)/shard_map/all_gather | solution.py:50
  201.6 82.9 %all-gather.5.cloned.1.call-start = ((), (), s32[]{:S(2)}) async-start(), calls=%async_computation.4 | async-start | bytes 5242880 | tf_op jit(solution)/shard_map/all_gather | solution.py:64
  235.2 6.1 %copy-start = (f32[1024,1024]{1,0:T(8,128)S(1)}, f32[1024,1024]{1,0:T(8,128)}, u32[]{:S(2)}) copy-start(f32[1024,1024]{1,0:T(8,128)} %all-gather.3.cloned.1.call-done) | copy-start | bytes 12582916
  245.1 39.3 %copy-start.1 = (bf16[512,1024]{1,0:T(8,128)(2,1)S(1)}, bf16[512,1024]{1,0:T(8,128)(2,1)}, u32[]{:S(2)}) copy-start(bf16[512,1024]{1,0:T(8,128)(2,1)} %param.2) | copy-start | bytes 3145732
Sparse Core Ops, SparseCore 0:
  58.9 44.6 reduce-scatter.1
  107.0 78.1 all-reduce.3
  201.7 33.4 all-gather.2
  250.0 34.4 all-gather.4
where the time goes:
time: 301 us
  waiting for transfers between devices  194 us (64%)
  blocking collectives  49.3 us (16%)
  matrix products  30.9 us (10%)
  between operations  15.3 us (5%)
  other arithmetic  7.97 us (3%)
    psum x1, waiting for transfers between devices, on_device(): own_rows = lax.psum(level_rows, 'wide')  81.6 us
    reduce_scatter x1, waiting for transfers between devices, narrow_rows(): return lax.psum_scatter(term, 'narrow', scatter_dimension=0, tiled=True)  44.7 us
    psum x1, blocking collectives, on_device(): count, sums = lax.psum((count_local, sums_local), ('wide', 'narrow'))  42.1 us
    all_gather x1, waiting for transfers between devices, on_device(): lax.all_gather(root_rows, 'narrow', axis=0, tiled=True)  34.6 us
    all_gather x1, waiting for transfers between devices, on_device(): root_full = lax.all_gather(root_rows, 'narrow', axis=0, tiled=True)  33.4 us
    dot_general x1, matrix products, on_device(): jnp.dot(centered_x, lax.all_gather(root_rows, 'narrow', axis=0, tiled=Tru...  9.62 us
    psum x1, blocking collectives, on_device(): trace_cov, square_sum = lax.psum((trace_part, square_part), 'narrow')  7.19 us
    dot_general x1, matrix products, on_device(): jnp.dot(base_rows, root_full, precision=lax.Precision.HIGHEST, preferred_...  6.13 us
  transfers between devices with their start and end apart: 4, of which 4 were waited for; matrix products, arithmetic and copies ran while one was open for 0% of the time, Pallas kernels for 0%

commit v1 on v0

--- a/solution.py
+++ b/solution.py
@@ -29,7 +29,7 @@
         masked, embeddings, (((0,), (0,)), ((), ())), preferred_element_type=jnp.float32
     )
     sums_local = jnp.dot(mask_half[None, :], embeddings, preferred_element_type=jnp.float32)[0]
-    count, sums = lax.psum((count_local, sums_local), ("wide", "narrow"))
+    count, sums = lax.psum(lax.psum((count_local, sums_local), "narrow"), "wide")
     term = shifted_scatter(gram, count_local, sums_local, sums / count)
     level_rows = narrow_rows(term)
     own_rows = lax.psum(level_rows, "wide")

time: 301 us -> 287 us (0.953)
  blocking collectives: 49.3 us -> 39 us
    psum x1 -> x2, blocking collectives: 42.1 us -> 31.8 us  [the longest x1 22.5 us: on_device(): lax.psum(lax.psum((count_local, sums_local), 'narrow'), 'wide')]
    reduce_scatter x1, waiting for transfers between devices: 44.7 us -> 40.9 us  [narrow_rows(): return lax.psum_scatter(term, 'narrow', scatter_dimension=0, tiled=True)]
where the time goes in v1:
time: 287 us; the launch traced here: 286 us
  waiting for transfers between devices  191 us (67%)
  blocking collectives  39 us (14%)
  matrix products  31 us (11%)
  between operations  15.3 us (5%)
  other arithmetic  7.97 us (3%)
    psum x1, waiting for transfers between devices, on_device(): own_rows = lax.psum(level_rows, 'wide')  81.6 us
    reduce_scatter x1, waiting for transfers between devices, narrow_rows(): return lax.psum_scatter(term, 'narrow', scatter_dimension=0, tiled=True)  40.9 us
    all_gather x1, waiting for transfers between devices, on_device(): lax.all_gather(root_rows, 'narrow', axis=0, tiled=True)  34.6 us
    all_gather x1, waiting for transfers between devices, on_device(): root_full = lax.all_gather(root_rows, 'narrow', axis=0, tiled=True)  33.4 us
    psum x1, blocking collectives, on_device(): lax.psum(lax.psum((count_local, sums_local), 'narrow'), 'wide')  22.5 us
    dot_general x1, matrix products, on_device(): jnp.dot(centered_x, lax.all_gather(root_rows, 'narrow', axis=0, tiled=Tru...  9.62 us
    psum x1, blocking collectives, on_device(): lax.psum((count_local, sums_local), 'narrow')  9.24 us
    psum x1, blocking collectives, on_device(): trace_cov, square_sum = lax.psum((trace_part, square_part), 'narrow')  7.19 us
  transfers between devices with their start and end apart: 4, of which 4 were waited for; matrix products, arithmetic and copies ran while one was open for 0% of the time, Pallas kernels for 0%

profile of v1, /device:TPU:0, one launch (start us, length us, event | category | flops | bytes accessed | tf_op | source)
XLA Modules:
  0.0 286.4 jit_solution(3160154486537890468)
XLA Ops:
  6.5 0.7 convert_element_type.14
  7.2 1.3 convert_reduce_fusion
  8.5 1.5 fusion.11
  10.0 9.2 %all-reduce.2 = (f32[1024]{0:T(1024)S(1)}, f32[]{:T(128)}) all-reduce(f32[1024]{0:T(1024)S(1)} %bitcast.12, f32[]{:T(128)} %convert_reduce_fusion), channel_id=1, replica_groups=mesh['wide'=8,'narrow'=4] {'narrow'}, use_global_device_ids=true, to_apply=%region_0.0 | all-reduce | flops 1025 | bytes 8200 | tf_op jit(solution)/shard_map/psum | solution.py:32
  19.2 22.5 %all-reduce = (f32[1024]{0:T(1024)S(1)}, f32[]{:T(128)}) all-reduce(f32[1024]{0:T(1024)S(1)} %get-tuple-element.9, f32[]{:T(128)} %get-tuple-element.10), channel_id=1, replica_groups=mesh['wide'=8,'narrow'=4] {'wide'}, use_global_device_ids=true, to_apply=%region_1.0 | all-reduce | flops 1025 | bytes 8200 | tf_op jit(solution)/shard_map/psum | solution.py:32
  41.8 1.3 broadcast_multiply_fusion
  43.0 5.3 %multiply_add_fusion = f32[1024,1024]{1,0:T(8,128)} fusion(bf16[512,1024]{1,0:T(8,128)(2,1)} %param.2, f32[1024]{0:T(1024)S(1)} %get-tuple-element.13, f32[1024]{0:T(1024)S(1)} %bitcast.13, f32[1024]{0:T(1024)S(1)} %get-tuple-element.14, bf16[512]{0:T(512)(128)(2,1)S(1)} %convert_element_type.14), kind=kOutput, calls=%fused_computation.1 | convolution fusion | flops 1080557568 | bytes 5256192 | tf_op jit(solution)/shard_map/dot_general | solution.py:28
  48.4 0.0 reduce-scatter.2.cloned.1.call-update
  48.4 0.0 all-reduce.5.cloned.1.call-start
  48.4 40.9 %reduce-scatter.2.cloned.1.call-done = f32[256,1024]{1,0:T(8,128)} async-done(((f32[1024,1024]{1,0:T(8,128)}), f32[256,1024]{1,0:T(8,128)}) %reduce-scatter.2.cloned.1.call-update) | async-done | bytes 1048592 | tf_op jit(solution)/shard_map/reduce_scatter | solution.py:17
  89.4 0.0 all-gather.3.cloned.1.call-start
  89.5 81.6 %all-reduce.5.cloned.1.call-done = f32[256,1024]{1,0:T(8,128)} async-done(((f32[256,1024]{1,0:T(8,128)}), f32[256,1024]{1,0:T(8,128)}) %all-reduce.5.cloned.1.call-update) | async-done | bytes 1048592 | tf_op jit(solution)/shard_map/psum | solution.py:35
  171.0 2.7 multiply_reduce_fusion
  173.8 2.3 gather_fusion
  176.2 0.7 reduce_sum.28
  176.8 7.2 %all-reduce.1 = (f32[]{:T(128)}, f32[]{:T(128)}) all-reduce(f32[]{:T(128)} %get-tuple-element.11, f32[]{:T(128)} %reduce_sum.28), channel_id=1, replica_groups=mesh['wide'=8,'narrow'=4] {'narrow'}, use_global_device_ids=true, to_apply=%region_10.11 | all-reduce | flops 2 | bytes 16 | tf_op jit(solution)/shard_map/psum | solution.py:45
  186.1 1.3 fusion.7
  187.4 0.2 all-gather.5.cloned.1.call-start
  187.7 33.4 %all-gather.3.cloned.1.call-done = f32[1024,1024]{1,0:T(8,128)} async-done(((f32[256,1024]{1,0:T(8,128)}), f32[1024,1024]{1,0:T(8,128)}) %all-gather.3.cloned.1.call-update) | async-done | bytes 4194320 | tf_op jit(solution)/shard_map/all_gather | solution.py:50
  221.1 6.1 %fusion.10 = f32[256,1024]{1,0:T(8,128)S(1)} fusion(f32[1024,1024]{1,0:T(8,128)} %all-gather.3.cloned.1.call-done, f32[256,1024]{1,0:T(8,128)S(1)} %get-tuple-element.12, f32[]{:T(128)S(6)} %sqrt.6, f32[]{:T(128)S(6)} %add.49, s32[256]{0:T(256)S(1)} %iota_add_fusion), kind=kOutput, calls=%fused_computation.23 | convolution fusion | flops 3222274048 | bytes 6292488 | tf_op jit(solution)/shard_map/dot_general | solution.py:51
  227.2 3.7 %fusion.4 = f32[256,1024]{1,0:T(8,128)S(1)} fusion(f32[256,1024]{1,0:T(8,128)S(1)} %fusion.10, f32[1024,1024]{1,0:T(8,128)S(1)} %copy-done, s32[256]{0:T(256)S(1)} %iota_add_fusion), kind=kOutput, calls=%fused_computation.9 | convolution fusion | flops 3222274048 | bytes 6292480 | tf_op jit(solution)/shard_map/dot_general | solution.py:54
  231.0 4.7 %fusion.12 = f32[256,1024]{1,0:T(8,128)} fusion(f32[256,1024]{1,0:T(8,128)S(1)} %fusion.4, f32[1024,1024]{1,0:T(8,128)S(1)} %copy-done), kind=kOutput, calls=%fused_computation.25 | convolution fusion | flops 3221225472 | bytes 6291456 | tf_op jit(solution)/shard_map/dot_general | solution.py:58
  235.7 34.6 %all-gather.5.cloned.1.call-done = f32[1024,1024]{1,0:T(8,128)} async-done(((f32[256,1024]{1,0:T(8,128)}), f32[1024,1024]{1,0:T(8,128)}) %all-gather.5.cloned.1.call-update) | async-done | bytes 4194320 | tf_op jit(solution)/shard_map/all_gather | solution.py:64
  270.3 9.6 %divide_convert_fusion = bf16[512,1024]{1,0:T(8,128)(2,1)} fusion(f32[1024,1024]{1,0:T(8,128)} %all-gather.5.cloned.1.call-done, bf16[512,1024]{1,0:T(8,128)(2,1)S(1)} %copy-done.1, f32[]{:T(128)S(6)} %sqrt.7, f32[1024]{0:T(1024)S(1)} %get-tuple-element.14), kind=kOutput, calls=%fused_computation.2 | convolution fusion | flops 6444548096 | bytes 6295556 | tf_op jit(solution)/shard_map/dot_general | solution.py:62
  (12 shorter events, 0.1 us)
Async XLA Ops:
  6.5 82.8 %reduce-scatter.2.cloned.1.call-start = ((), (), s32[]{:S(2)}) async-start(), calls=%async_computation.1 | async-start | bytes 5242880 | tf_op jit(solution)/shard_map/reduce_scatter | solution.py:17
  48.4 122.7 %all-reduce.5.cloned.1.call-start = ((), (), s32[]{:S(2)}) async-start(), calls=%async_computation.2 | async-start | bytes 2097152 | tf_op jit(solution)/shard_map/psum | solution.py:35
  89.4 131.7 %all-gather.3.cloned.1.call-start = ((), (), s32[]{:S(2)}) async-start(), calls=%async_computation.3 | async-start | bytes 5242880 | tf_op jit(solution)/shard_map/all_gather | solution.py:50
  187.4 82.9 %all-gather.5.cloned.1.call-start = ((), (), s32[]{:S(2)}) async-start(), calls=%async_computation.4 | async-start | bytes 5242880 | tf_op jit(solution)/shard_map/all_gather | solution.py:64
  221.1 6.1 %copy-start = (f32[1024,1024]{1,0:T(8,128)S(1)}, f32[1024,1024]{1,0:T(8,128)}, u32[]{:S(2)}) copy-start(f32[1024,1024]{1,0:T(8,128)} %all-gather.3.cloned.1.call-done) | copy-start | bytes 12582916
  231.0 39.3 %copy-start.1 = (bf16[512,1024]{1,0:T(8,128)(2,1)S(1)}, bf16[512,1024]{1,0:T(8,128)(2,1)}, u32[]{:S(2)}) copy-start(bf16[512,1024]{1,0:T(8,128)(2,1)} %param.2) | copy-start | bytes 3145732
Sparse Core Ops, SparseCore 0:
  48.5 40.8 reduce-scatter.1
  92.9 78.1 all-reduce.4
  187.5 33.4 all-gather.2
  235.8 34.4 all-gather.4
